TPU v7x, 256 devices: a whole 4x4x8 slice. The times are simulated.
256 devices in a mesh: op: 4 (over x), sec: 64 (over z, y, core).
Axes of the slice: x: 4, y: 4, z: 8, core: 2. Of those that a mesh axis runs over, the one named last changes fastest.
Arguments:
- wavefunction: bfloat16 [4096, 128, 128], P('sec'), may hold values from -6 to 6
- left_ops: bfloat16 [2, 16, 8, 128, 128], P(None, 'op'), may hold values from -0.5 to 0.5
- right_ops: bfloat16 [2, 16, 8, 128, 128], P(None, 'op'), may hold values from -0.09375 to 0.09375
- left_sector: int32 [4096], P('sec'), may hold values from 0 to 7
- right_sector: int32 [4096], P('sec'), may hold values from 0 to 7
- target: int32 [2, 4096], replicated, may hold values from 0 to 4095, as said below
Outputs:
- applied_blocks: float32 [4096, 128, 128], P('sec', 'op')
Inputs may be any that keep to these rules, and one draw needn't show every extreme that they name: For every class, target is a permutation of the 4096 blocks; block b lies on index b // 64 of sec, and for every class exactly 1 of the blocks of one index of sec map to blocks of each index of sec.
All inputs are finite; a program needn't handle non-finite values.
Results may differ from a plain program's by a relative error of at most 0.0029.
Values may be sent and summed in bfloat16 or wider, within the bound.
No kernel may reach another device: no remote copies, remote signals or barrier semaphores. Data moves between devices by JAX's collectives and lax.ppermute only.
A program may use at most 64 MiB of HBM per device.

v0:
```python
import jax
import jax.numpy as jnp
from jax import lax
from jax.sharding import PartitionSpec as P


def class_terms(initial, left_ops, right_ops, wavefunction, left_sector, right_sector):

    def add_term(running, operators):
        left_term, right_term = operators
        left_blocks = jnp.take(left_term, left_sector, axis=0)
        left_mixed = jnp.einsum(
            "bij,bjk->bik", left_blocks, wavefunction, preferred_element_type=jnp.float32
        ).astype(jnp.bfloat16)
        right_blocks = jnp.take(right_term, right_sector, axis=0)
        return (
            running
            + jnp.einsum(
                "bik,blk->bil", left_mixed, right_blocks, preferred_element_type=jnp.float32
            ),
            None,
        )

    running, _ = lax.scan(add_term, initial, (left_ops, right_ops))
    return running


def routing(target_row, blocks_here, own_index, shards):
    slots = blocks_here // shards
    dest_device = (target_row // blocks_here).reshape(shards, blocks_here)
    dest_slot = (target_row % blocks_here).reshape(shards, blocks_here)
    slot_ids = jnp.arange(blocks_here, dtype=jnp.int32)
    same_dest = dest_device[:, :, None] == dest_device[:, None, :]
    earlier = slot_ids[None, :] < slot_ids[:, None]
    rank_in = jnp.sum((same_dest & earlier[None, :, :]).astype(jnp.int32), axis=2)
    position = dest_device * slots + rank_in
    own_position = lax.dynamic_index_in_dim(position, own_index, 0, keepdims=False)
    send_index = jnp.sum(
        jnp.where(own_position[None, :] == slot_ids[:, None], slot_ids[None, :], 0), axis=1
    )
    source = jnp.arange(shards, dtype=jnp.int32)[:, None]
    arrival = source * slots + rank_in
    for_here = dest_device == own_index
    arrives_here = for_here[:, :, None] & (dest_slot[:, :, None] == slot_ids[None, None, :])
    recv_index = jnp.sum(jnp.where(arrives_here, arrival[:, :, None], 0), axis=(0, 1))
    return (send_index, recv_index)


def per_device(wavefunction, left_ops, right_ops, left_sector, right_sector, target):
    shards = lax.axis_size("sec")
    own_index = lax.axis_index("sec")
    blocks_here = wavefunction.shape[0]
    classes = target.shape[0]
    empty = jnp.zeros(wavefunction.shape, jnp.float32)
    partial_sum = jnp.zeros(wavefunction.shape, jnp.float32)
    for class_index in range(classes):
        summed = class_terms(
            empty,
            left_ops[class_index],
            right_ops[class_index],
            wavefunction,
            left_sector,
            right_sector,
        )
        send_index, recv_index = routing(target[class_index], blocks_here, own_index, shards)
        arrived = lax.all_to_all(
            jnp.take(summed, send_index, axis=0), "sec", split_axis=0, concat_axis=0, tiled=True
        )
        partial_sum = partial_sum + jnp.take(arrived, recv_index, axis=0)
    return lax.psum_scatter(partial_sum, "op", scatter_dimension=1, tiled=True)


def solution(mesh):
    in_specs = (
        P("sec", None, None),
        P(None, "op", None, None, None),
        P(None, "op", None, None, None),
        P("sec"),
        P("sec"),
        P(),
    )
    out_specs = P("sec", "op", None)
    return jax.shard_map(
        per_device, mesh=mesh, in_specs=in_specs, out_specs=out_specs, check_vma=False
    )
```

profile of v0, /device:TPU:1, one launch (start us, length us, event | category | flops | bytes accessed | tf_op | source)
XLA Modules:
  0.0 346.5 jit_solution(8253279121539807352)
XLA Ops:
  7.7 3.7 %convert_reduce_fusion.1 = (s32[64,64]{1,0:T(8,128)S(1)}, s32[64,64]{1,0:T(8,128)S(1)}) fusion(s32[64,64]{1,0:T(8,128)S(1)} %get-tuple-element.164, pred[64,64]{1,0:T(8,128)(4,1)S(1)} %iota_compare_fusion.4, s32[64,64]{1,0:T(8,128)S(1)} %get-tuple-element.166), kind=kLoop, calls=%fused_computation.50 | loop fusion | flops 2088960 | bytes 69632 | tf_op jit(solution)/shard_map/reduce_sum | solution.py:35
  11.7 4.4 %slice_bitcast_fusion.2 = (bf16[4,8,128,128]{3,2,1,0:T(8,128)(2,1)}, bf16[4,8,128,128]{3,2,1,0:T(8,128)(2,1)}, bf16[4,8,128,128]{3,2,1,0:T(8,128)(2,1)}, bf16[4,8,128,128]{3,2,1,0:T(8,128)(2,1)}) fusion(bf16[2,4,8,128,128]{4,3,2,1,0:T(8,128)(2,1)} %param.16, bf16[2,4,8,128,128]{4,3,2,1,0:T(8,128)(2,1)} %param.15), kind=kLoop, calls=%fused_computation.55 | loop fusion | bytes 8388608 | tf_op jit(solution)/shard_map/squeeze | solution.py:60
  16.1 46.2 %while.23 = (s32[]{:T(128)}, f32[64,128,128]{2,1,0:T(8,128)}, bf16[4,8,128,128]{3,2,1,0:T(8,128)(2,1)}, s32[64]{0:T(128)S(1)}, bf16[64,128,128]{2,1,0:T(8,128)(2...) while((s32[]{:T(128)}, f32[64,128,128]{2,1,0:T(8,128)}, ...), condition=%wide.region_6.9_spmd.clone, body=%wide.region_5.8_spmd.clone.sunk | while | flops 542116992 | bytes 24128372 | solution.py:24
  18.2 2.1 gather_fusion.3
  20.4 6.4 %select_add_fusion.6 = f32[64,128,128]{2,1,0:T(8,128)} fusion(f32[64,128,128]{2,1,0:T(8,128)} %get-tuple-element.311, bf16[64,128,128]{2,1,0:T(8,128)(2,1)S(1)} %gather_fusion.2, pred[64]{0:T(512)(128)(4,1)S(1)} %get-tuple-element.297, pred[]{:T(512)S(6)} %compare.51, bf16[64,128,128]{2,1,0:T(8,128)(2,1)} %get-tuple-element.323, ...), kind=kOutput, calls=%fused_computation.25.clone.1 | convolution fusion | flops 542113792 | bytes 14680193 | tf_op jit(solution)/shard_map/while/body/eval_jaxpr/bik,blk->bil/dot_general | solution.py:18
  28.8 2.1 gather_fusion.3
  31.0 7.6 %select_add_fusion.6 = f32[64,128,128]{2,1,0:T(8,128)} fusion(f32[64,128,128]{2,1,0:T(8,128)} %get-tuple-element.311, bf16[64,128,128]{2,1,0:T(8,128)(2,1)S(1)} %gather_fusion.2, pred[64]{0:T(512)(128)(4,1)S(1)} %get-tuple-element.297, pred[]{:T(512)S(6)} %compare.51, bf16[64,128,128]{2,1,0:T(8,128)(2,1)} %get-tuple-element.323, ...), kind=kOutput, calls=%fused_computation.25.clone.1 | convolution fusion | flops 542113792 | bytes 14680193 | tf_op jit(solution)/shard_map/while/body/eval_jaxpr/bik,blk->bil/dot_general | solution.py:18
  42.8 7.6 %select_add_fusion.6 = f32[64,128,128]{2,1,0:T(8,128)} fusion(f32[64,128,128]{2,1,0:T(8,128)} %get-tuple-element.311, bf16[64,128,128]{2,1,0:T(8,128)(2,1)S(1)} %gather_fusion.2, pred[64]{0:T(512)(128)(4,1)S(1)} %get-tuple-element.297, pred[]{:T(512)S(6)} %compare.51, bf16[64,128,128]{2,1,0:T(8,128)(2,1)} %get-tuple-element.323, ...), kind=kOutput, calls=%fused_computation.25.clone.1 | convolution fusion | flops 542113792 | bytes 14680193 | tf_op jit(solution)/shard_map/while/body/eval_jaxpr/bik,blk->bil/dot_general | solution.py:18
  54.7 7.6 %select_add_fusion.6 = f32[64,128,128]{2,1,0:T(8,128)} fusion(f32[64,128,128]{2,1,0:T(8,128)} %get-tuple-element.311, bf16[64,128,128]{2,1,0:T(8,128)(2,1)S(1)} %gather_fusion.2, pred[64]{0:T(512)(128)(4,1)S(1)} %get-tuple-element.297, pred[]{:T(512)S(6)} %compare.51, bf16[64,128,128]{2,1,0:T(8,128)(2,1)} %get-tuple-element.323, ...), kind=kOutput, calls=%fused_computation.25.clone.1 | convolution fusion | flops 542113792 | bytes 14680193 | tf_op jit(solution)/shard_map/while/body/eval_jaxpr/bik,blk->bil/dot_general | solution.py:18
  62.3 5.0 %gather_fusion.6 = f32[64,128,128]{2,1,0:T(8,128)} fusion(f32[64,128,128]{2,1,0:T(8,128)} %get-tuple-element.82, s32[1024]{0:T(1024)S(1)} %pad_clamp_fusion.5), kind=kCustom, calls=%fused_computation.6.clone | custom fusion | bytes 8388864 | tf_op jit(solution)/shard_map/jit(_take)/gather | solution.py:67
  67.3 4.5 %broadcast_select_fusion = f32[64,128,128]{2,1,0:T(8,128)} fusion(f32[64,128,128]{2,1,0:T(8,128)} %gather_fusion.6, pred[64]{0:T(512)(128)(4,1)S(1)} %get-tuple-element.187), kind=kLoop, calls=%fused_computation.43 | loop fusion | flops 1048576 | bytes 8388672 | tf_op jit(solution)/shard_map/jit(_take)/select_n | solution.py:67
  71.8 13.3 %all-to-all-start.1 = ((f32[64,128,128]{2,1,0:T(8,128)}), f32[64,128,128]{2,1,0:T(8,128)}, u32[]{:S(2)}, u32[]{:S(2)}) async-start(f32[64,128,128]{2,1,0:T(8,128)} %broadcast_select_fusion), calls=%async_computation.1 | async-start | bytes 8388608 | tf_op jit(solution)/shard_map/all_to_all | solution.py:66
  85.2 46.5 %while.22 = (s32[]{:T(128)}, f32[64,128,128]{2,1,0:T(8,128)}, bf16[4,8,128,128]{3,2,1,0:T(8,128)(2,1)}, s32[64]{0:T(128)S(1)}, bf16[64,128,128]{2,1,0:T(8,128)(2...) while((s32[]{:T(128)}, f32[64,128,128]{2,1,0:T(8,128)}, ...), condition=%wide.region_1.0_spmd.clone, body=%wide.region_0.2_spmd.clone.sunk | while | flops 542116992 | bytes 24128372 | solution.py:24
  87.3 2.2 gather_fusion.1
  89.4 6.4 %select_add_fusion.5 = f32[64,128,128]{2,1,0:T(8,128)} fusion(f32[64,128,128]{2,1,0:T(8,128)} %get-tuple-element.338, bf16[64,128,128]{2,1,0:T(8,128)(2,1)S(1)} %gather_fusion, pred[64]{0:T(512)(128)(4,1)S(1)} %get-tuple-element.284, pred[]{:T(512)S(6)} %compare.50, bf16[64,128,128]{2,1,0:T(8,128)(2,1)} %get-tuple-element.350, ...), kind=kOutput, calls=%fused_computation.8.clone.1 | convolution fusion | flops 542113792 | bytes 14680193 | tf_op jit(solution)/shard_map/while/body/eval_jaxpr/bik,blk->bil/dot_general | solution.py:18
  98.0 2.2 gather_fusion.1
  100.1 7.7 %select_add_fusion.5 = f32[64,128,128]{2,1,0:T(8,128)} fusion(f32[64,128,128]{2,1,0:T(8,128)} %get-tuple-element.338, bf16[64,128,128]{2,1,0:T(8,128)(2,1)S(1)} %gather_fusion, pred[64]{0:T(512)(128)(4,1)S(1)} %get-tuple-element.284, pred[]{:T(512)S(6)} %compare.50, bf16[64,128,128]{2,1,0:T(8,128)(2,1)} %get-tuple-element.350, ...), kind=kOutput, calls=%fused_computation.8.clone.1 | convolution fusion | flops 542113792 | bytes 14680193 | tf_op jit(solution)/shard_map/while/body/eval_jaxpr/bik,blk->bil/dot_general | solution.py:18
  109.9 2.2 gather_fusion.1
  112.1 7.7 %select_add_fusion.5 = f32[64,128,128]{2,1,0:T(8,128)} fusion(f32[64,128,128]{2,1,0:T(8,128)} %get-tuple-element.338, bf16[64,128,128]{2,1,0:T(8,128)(2,1)S(1)} %gather_fusion, pred[64]{0:T(512)(128)(4,1)S(1)} %get-tuple-element.284, pred[]{:T(512)S(6)} %compare.50, bf16[64,128,128]{2,1,0:T(8,128)(2,1)} %get-tuple-element.350, ...), kind=kOutput, calls=%fused_computation.8.clone.1 | convolution fusion | flops 542113792 | bytes 14680193 | tf_op jit(solution)/shard_map/while/body/eval_jaxpr/bik,blk->bil/dot_general | solution.py:18
  121.8 2.2 gather_fusion.1
  124.0 7.7 %select_add_fusion.5 = f32[64,128,128]{2,1,0:T(8,128)} fusion(f32[64,128,128]{2,1,0:T(8,128)} %get-tuple-element.338, bf16[64,128,128]{2,1,0:T(8,128)(2,1)S(1)} %gather_fusion, pred[64]{0:T(512)(128)(4,1)S(1)} %get-tuple-element.284, pred[]{:T(512)S(6)} %compare.50, bf16[64,128,128]{2,1,0:T(8,128)(2,1)} %get-tuple-element.350, ...), kind=kOutput, calls=%fused_computation.8.clone.1 | convolution fusion | flops 542113792 | bytes 14680193 | tf_op jit(solution)/shard_map/while/body/eval_jaxpr/bik,blk->bil/dot_general | solution.py:18
  131.7 5.0 %gather_fusion.4 = f32[64,128,128]{2,1,0:T(8,128)} fusion(f32[64,128,128]{2,1,0:T(8,128)} %get-tuple-element.81, s32[1024]{0:T(1024)S(1)} %pad_clamp_fusion.7), kind=kCustom, calls=%fused_computation.1.clone | custom fusion | bytes 8388864 | tf_op jit(solution)/shard_map/jit(_take)/gather | solution.py:67
  136.6 4.5 %broadcast_select_fusion.1 = f32[64,128,128]{2,1,0:T(8,128)} fusion(f32[64,128,128]{2,1,0:T(8,128)} %gather_fusion.4, pred[64]{0:T(512)(128)(4,1)S(1)} %get-tuple-element.188), kind=kLoop, calls=%fused_computation.44 | loop fusion | flops 1048576 | bytes 8388672 | tf_op jit(solution)/shard_map/jit(_take)/select_n | solution.py:67
  141.1 38.7 %all-to-all-done.1 = f32[64,128,128]{2,1,0:T(8,128)} async-done(((f32[64,128,128]{2,1,0:T(8,128)}), f32[64,128,128]{2,1,0:T(8,128)}, u32[]{:S(2)}, u32[]{:S(2)}) %all-to-all-start.1) | async-done | bytes 4194336 | tf_op jit(solution)/shard_map/all_to_all | solution.py:66
  179.8 7.1 %all-to-all-start = ((f32[64,128,128]{2,1,0:T(8,128)}), f32[64,128,128]{2,1,0:T(8,128)}, u32[]{:S(2)}, u32[]{:S(2)}) async-start(f32[64,128,128]{2,1,0:T(8,128)} %broadcast_select_fusion.1), calls=%async_computation | async-start | bytes 8388608 | tf_op jit(solution)/shard_map/all_to_all | solution.py:66
  187.0 2.3 select_reduce_fusion
  189.4 2.3 select_reduce_fusion.1
  191.7 5.0 %gather_fusion.7 = f32[64,128,128]{2,1,0:T(8,128)} fusion(f32[64,128,128]{2,1,0:T(8,128)} %all-to-all-done.1, s32[1024]{0:T(1024)S(1)} %pad_clamp_fusion.4), kind=kCustom, calls=%fused_computation.7.clone | custom fusion | bytes 8388864 | tf_op jit(solution)/shard_map/jit(_take)/gather | solution.py:69
  196.7 85.2 %all-to-all-done = f32[64,128,128]{2,1,0:T(8,128)} async-done(((f32[64,128,128]{2,1,0:T(8,128)}), f32[64,128,128]{2,1,0:T(8,128)}, u32[]{:S(2)}, u32[]{:S(2)}) %all-to-all-start) | async-done | bytes 4194336 | tf_op jit(solution)/shard_map/all_to_all | solution.py:66
  281.9 4.9 %gather_fusion.5 = f32[64,128,128]{2,1,0:T(8,128)} fusion(f32[64,128,128]{2,1,0:T(8,128)} %all-to-all-done, s32[1024]{0:T(1024)S(1)} %pad_clamp_fusion.6), kind=kCustom, calls=%fused_computation.5.clone | custom fusion | bytes 8388864 | tf_op jit(solution)/shard_map/jit(_take)/gather | solution.py:69
  286.8 6.0 %select_add_fusion.2 = f32[64,128,128]{2,1,0:T(8,128)} fusion(f32[64,128,128]{2,1,0:T(8,128)} %gather_fusion.7, f32[64,128,128]{2,1,0:T(8,128)} %gather_fusion.5, pred[64]{0:T(512)(128)(4,1)S(1)} %get-tuple-element.185, pred[64]{0:T(512)(128)(4,1)S(1)} %get-tuple-element.186), kind=kLoop, calls=%fused_computation.42 | loop fusion | flops 3145728 | bytes 12583040 | tf_op jit(solution)/shard_map/add | solution.py:69
  292.8 46.8 %reduce-scatter.2.cloned.1.call-done = f32[64,32,128]{2,1,0:T(8,128)} async-done(((f32[64,128,128]{2,1,0:T(8,128)}), f32[64,32,128]{2,1,0:T(8,128)}) %reduce-scatter.2.cloned.1.call-update) | async-done | bytes 1048592 | tf_op jit(solution)/shard_map/reduce_scatter | solution.py:70
  (81 shorter events, 22.2 us)
Async XLA Ops:
  11.7 4.4 %copy-start = (s32[64]{0:T(128)S(1)}, s32[64]{0:T(128)}, u32[]{:S(2)}) copy-start(s32[64]{0:T(128)} %param.17) | copy-start | bytes 772
  11.7 4.4 %copy-start.1 = (s32[64]{0:T(128)S(1)}, s32[64]{0:T(128)}, u32[]{:S(2)}) copy-start(s32[64]{0:T(128)} %param.18) | copy-start | bytes 772
  71.8 108.1 %all-to-all-start.1 = ((f32[64,128,128]{2,1,0:T(8,128)}), f32[64,128,128]{2,1,0:T(8,128)}, u32[]{:S(2)}, u32[]{:S(2)}) async-start(f32[64,128,128]{2,1,0:T(8,128)} %broadcast_select_fusion), calls=%async_computation.1 | async-start | bytes 8388608 | tf_op jit(solution)/shard_map/all_to_all | solution.py:66
  179.8 102.0 %all-to-all-start = ((f32[64,128,128]{2,1,0:T(8,128)}), f32[64,128,128]{2,1,0:T(8,128)}, u32[]{:S(2)}, u32[]{:S(2)}) async-start(f32[64,128,128]{2,1,0:T(8,128)} %broadcast_select_fusion.1), calls=%async_computation | async-start | bytes 8388608 | tf_op jit(solution)/shard_map/all_to_all | solution.py:66
  187.0 152.7 %reduce-scatter.2.cloned.1.call-start = ((), (), s32[]{:S(2)}) async-start(), calls=%async_computation.3 | async-start | bytes 5242880 | tf_op jit(solution)/shard_map/reduce_scatter | solution.py:70
Sparse Core Ops, SparseCore 0:
  293.0 46.6 reduce-scatter.1
where the time goes:
time: 347 us
  waiting for transfers between devices  171 us (49%)
  local copies, waits for them, and re-layouts  58.7 us (17%)
  matrix products  58.7 us (17%)
  other arithmetic  23.9 us (7%)
  starting transfers between devices  20.5 us (6%)
  between operations  13.6 us (4%)
    all_to_all x2, waiting for transfers between devices, per_device(): lax.all_to_all(jnp.take(summed, send_index, axis=0), 'sec', split_axis=0,...  124 us
    dot_general x8, matrix products, add_term(): jnp.einsum('bik,blk->bil', left_mixed, right_blocks, preferred_element_ty...  58.7 us
    reduce_scatter x1, waiting for transfers between devices, per_device(): return lax.psum_scatter(partial_sum, 'op', scatter_dimension=1, tiled=True)  46.8 us
    all_to_all x2, starting transfers between devices, per_device(): lax.all_to_all(jnp.take(summed, send_index, axis=0), 'sec', split_axis=0,...  20.4 us
    gather x8, local copies, waits for them, and re-layouts, add_term(): left_blocks = jnp.take(left_term, left_sector, axis=0)  17.3 us
    gather x2, local copies, waits for them, and re-layouts, per_device(): jnp.take(summed, send_index, axis=0)  9.93 us
    gather x2, local copies, waits for them, and re-layouts, per_device(): partial_sum = partial_sum + jnp.take(arrived, recv_index, axis=0)  9.9 us
    select_n x3, other arithmetic, per_device(): jnp.take(summed, send_index, axis=0)  9 us
  transfers between devices with their start and end apart: 3, of which 3 were waited for; matrix products, arithmetic and copies ran while one was open for 19% of the time, Pallas kernels for 0%

commit v1 on v0

v1 whole, which is shorter than its diff:
```python
import functools

import jax
import jax.numpy as jnp
from jax import lax
from jax.experimental import pallas as pl
from jax.experimental.pallas import tpu as pltpu
from jax.sharding import PartitionSpec as P

F32, BF16 = jnp.float32, jnp.bfloat16


def apply_kernel(op_ref, target_ref, lsec_ref, rsec_ref, wave_ref, left_ref, right_ref, *outs, chunk, shards_of, per):
    terms, rows = left_ref.shape[1], left_ref.shape[3]
    op_size = rows // per
    half = per // 2
    own_op = op_ref[0]
    base = pl.program_id(0) * chunk
    offsets = [pl.multiple_of(lax.rem(own_op + r, op_size) * per, per) for r in range(op_size)]

    def one(i):
        b = base + i
        ls, rs = lsec_ref[b], rsec_ref[b]
        place = target_ref[b] // shards_of
        w = wave_ref[i]
        stacked = jnp.concatenate(
            [left_ref[0, t, ls, pl.ds(off, per), :] for t in range(terms) for off in offsets], axis=0
        )
        mixed = jnp.dot(stacked, w, preferred_element_type=F32).astype(BF16)
        lhs = jnp.concatenate([mixed[t * rows : (t + 1) * rows] for t in range(terms)], axis=1)
        rhs = jnp.concatenate([right_ref[0, t, rs] for t in range(terms)], axis=1)
        acc = lax.dot_general(lhs, rhs, (((1,), (1,)), ((), ())), preferred_element_type=F32)
        outs[0][place] = acc[:per]
        for k, out in enumerate(outs[1:]):
            lo = per + k * half
            out[place] = acc[lo : lo + half].astype(BF16)

    def body(i, carry):
        one(i)
        return carry

    lax.fori_loop(0, chunk, body, 0, unroll=2)


def apply_class(q, own_op, own_target, left_sector, right_sector, wavefunction, left_ops, right_ops):
    blocks, rows, cols = wavefunction.shape
    _, terms, sectors, _, _ = left_ops.shape
    op_size = lax.axis_size("op")
    per = rows // op_size
    chunk = 16
    ops_block = (1, terms, sectors, rows, rows)
    rops_block = (1, terms, right_ops.shape[2], cols, cols)
    outs = [jax.ShapeDtypeStruct((blocks, per, cols), F32)] + [
        jax.ShapeDtypeStruct((blocks, per // 2, cols), BF16) for _ in range(2 * (op_size - 1))
    ]
    flops = 2 * blocks * terms * (rows * rows * cols + rows * cols * cols)
    return pl.pallas_call(
        functools.partial(apply_kernel, chunk=chunk, shards_of=blocks, per=per),
        out_shape=outs,
        grid_spec=pltpu.PrefetchScalarGridSpec(
            num_scalar_prefetch=4,
            grid=(blocks // chunk,),
            in_specs=[
                pl.BlockSpec((chunk, rows, cols), lambda g, *_: (g, 0, 0)),
                pl.BlockSpec(ops_block, lambda g, *_: (q, 0, 0, 0, 0)),
                pl.BlockSpec(rops_block, lambda g, *_: (q, 0, 0, 0, 0)),
            ],
            out_specs=[pl.BlockSpec(o.shape, lambda g, *_: (0, 0, 0)) for o in outs],
        ),
        cost_estimate=pl.CostEstimate(flops=flops, bytes_accessed=8 << 20, transcendentals=0),
        name=f"apply_class_{q}",
    )(own_op, own_target[q], left_sector, right_sector, wavefunction, left_ops, right_ops)


def place_kernel(slot_ref, arrived_ref, out_ref):
    sources, classes = arrived_ref.shape[:2]
    for q in range(classes):

        def body(s, carry):
            slot = slot_ref[q, s]
            block = arrived_ref[s, q].astype(F32)
            out_ref[slot] = block if q == 0 else out_ref[slot] + block
            return carry

        lax.fori_loop(0, sources, body, 0, unroll=4)


def op_exchange(parts, up, down):
    own, o1a, o1b, o2a, o2b, o3a, o3b = parts
    half = o1a.shape[1]
    ra, rb = up(o2a), down(o2b)
    q1, q3 = up(o1b), down(o3a)
    ca = up((o1a.astype(F32) + ra.astype(F32)).astype(BF16))
    cb = down((o3b.astype(F32) + rb.astype(F32)).astype(BF16))
    top = own[:, :half] + q3.astype(F32) + ca.astype(F32)
    bottom = own[:, half:] + q1.astype(F32) + cb.astype(F32)
    return jnp.concatenate([top, bottom], axis=1).astype(BF16)


def per_device(wavefunction, left_ops, right_ops, left_sector, right_sector, target):
    shards = lax.axis_size("sec")
    op_size = lax.axis_size("op")
    own_sec, own_op = lax.axis_index("sec"), lax.axis_index("op")
    blocks, rows, cols = wavefunction.shape
    classes = target.shape[0]
    own_target = lax.dynamic_slice(target, (0, own_sec * blocks), (classes, blocks))
    op_scalar = own_op.astype(jnp.int32).reshape(1)
    by_source = target.reshape(classes, shards, blocks)
    slots = jnp.sum(jnp.where(by_source // blocks == own_sec, by_source % blocks, 0), axis=2)
    up = functools.partial(lax.ppermute, axis_name="op", perm=[(i, (i + 1) % op_size) for i in range(op_size)])
    down = functools.partial(lax.ppermute, axis_name="op", perm=[(i, (i - 1) % op_size) for i in range(op_size)])
    sums = []
    for q in range(classes):
        parts = apply_class(q, op_scalar, own_target, left_sector, right_sector, wavefunction, left_ops, right_ops)
        sums.append(op_exchange(parts, up, down))
    arrived = lax.all_to_all(jnp.stack(sums, axis=1), "sec", split_axis=0, concat_axis=0, tiled=True)
    per = rows // op_size
    return pl.pallas_call(
        place_kernel,
        out_shape=jax.ShapeDtypeStruct((blocks, per, cols), F32),
        grid_spec=pltpu.PrefetchScalarGridSpec(
            num_scalar_prefetch=1,
            grid=(1,),
            in_specs=[pl.BlockSpec(arrived.shape, lambda g, *_: (0, 0, 0, 0))],
            out_specs=pl.BlockSpec((blocks, per, cols), lambda g, *_: (0, 0, 0)),
        ),
        name="place_blocks",
    )(slots, arrived)


def solution(mesh):
    in_specs = (
        P("sec", None, None),
        P(None, "op", None, None, None),
        P(None, "op", None, None, None),
        P("sec"),
        P("sec"),
        P(),
    )
    return jax.shard_map(
        per_device, mesh=mesh, in_specs=in_specs, out_specs=P("sec", "op", None), check_vma=False
    )
```

time: 347 us -> 115 us (0.33)
  waiting for transfers between devices: 171 us -> 43.3 us
  matrix products: 58.7 us -> 0 us
  local copies, waits for them, and re-layouts: 58.7 us -> 2.46 us
  Pallas kernels: 0 us -> 36.8 us
  other arithmetic: 23.9 us -> 3.48 us
  between operations: 13.6 us -> 0.17 us
  starting transfers between devices: 20.5 us -> 28.5 us
    all_to_all x2 -> x1, waiting for transfers between devices: 124 us -> 27.3 us  [per_device(): lax.all_to_all(jnp.stack(sums, axis=1), 'sec', split_axis=0, concat_axis=...]
    dot_general x8 -> x0, matrix products: 58.7 us -> none  [add_term(): jnp.einsum('bik,blk->bil', left_mixed, right_blocks, preferred_element_ty...]
    reduce_scatter x1 -> x0, waiting for transfers between devices: 46.8 us -> none  [per_device(): return lax.psum_scatter(partial_sum, 'op', scatter_dimension=1, tiled=True)]
    gather x20 -> x0, local copies, waits for them, and re-layouts: 44.7 us -> none  [the longest x8 17.3 us: add_term(): left_blocks = jnp.take(left_term, left_sector, axis=0)]
    pallas_call x0 -> x3, Pallas kernels: none -> 36.8 us  [the longest x2 33.5 us: apply_class(): pl.pallas_call(functools.partial(apply_kernel, chunk=chunk, shards_of=blo...]
    ppermute x0 -> x12, waiting for transfers between devices: none -> 16 us  [the longest x4 5.43 us: op_exchange(): q1, q3 = (up(o1b), down(o3a))]
    ppermute x0 -> x12, starting transfers between devices: none -> 13.7 us  [the longest x4 6.02 us: op_exchange(): ra, rb = (up(o2a), down(o2b))]
    squeeze x11 -> x1, local copies, waits for them, and re-layouts: 13 us -> 0.57 us  [apply_class(): own_target[q]]
  transfers between devices with their start and end apart: 3 -> 13, of which waited for: 3 -> 7; matrix products, arithmetic and copies ran while one was open for 19% -> 2% of each run, Pallas kernels for 0% -> 15%
where the time goes in v1:
time: 115 us
  waiting for transfers between devices  43.3 us (38%)
  Pallas kernels  36.8 us (32%)
  starting transfers between devices  28.5 us (25%)
  other arithmetic  3.48 us (3%)
  local copies, waits for them, and re-layouts  2.46 us (2%)
    pallas_call x2, Pallas kernels, apply_class(): pl.pallas_call(functools.partial(apply_kernel, chunk=chunk, shards_of=blo...  33.5 us
    all_to_all x1, waiting for transfers between devices, per_device(): lax.all_to_all(jnp.stack(sums, axis=1), 'sec', split_axis=0, concat_axis=...  27.3 us
    all_to_all x1, starting transfers between devices, per_device(): lax.all_to_all(jnp.stack(sums, axis=1), 'sec', split_axis=0, concat_axis=...  14.8 us
    ppermute x4, starting transfers between devices, op_exchange(): ra, rb = (up(o2a), down(o2b))  6.02 us
    ppermute x4, waiting for transfers between devices, op_exchange(): q1, q3 = (up(o1b), down(o3a))  5.43 us
    ppermute x2, starting transfers between devices, op_exchange(): cb = down((o3b.astype(F32) + rb.astype(F32)).astype(BF16))  4.54 us
    ppermute x2, waiting for transfers between devices, op_exchange(): cb = down((o3b.astype(F32) + rb.astype(F32)).astype(BF16))  4.04 us
    ppermute x4, waiting for transfers between devices, op_exchange(): ra, rb = (up(o2a), down(o2b))  3.7 us
  transfers between devices with their start and end apart: 13, of which 7 were waited for; matrix products, arithmetic and copies ran while one was open for 2% of the time, Pallas kernels for 15%

profile of v1, /device:TPU:1, one launch (start us, length us, event | category | flops | bytes accessed | tf_op | source)
XLA Modules:
  0.0 114.8 jit_solution(3433794375317631102)
XLA Ops:
  0.0 0.7 constant_dynamic-slice_fusion
  0.8 0.6 slice_bitcast_fusion.1
  1.3 16.7 %apply_class_0.1 = (f32[64,32,128]{2,1,0:T(8,128)}, bf16[64,16,128]{2,1,0:T(8,128)(2,1)}, bf16[64,16,128]{2,1,0:T(8,128)(2,1)}, bf16[64,16,128]{2,1,0:T(8,128)(2...) custom-call(s32[1]{0:T(128)} %bitcast.op_ref, ...), custom_call_target="tpu_custom_call" | custom-call | flops 2147483648 | bytes 8388608 | tf_op jit(solution)/shard_map/apply_class_0/pallas_call | solution.py:57
  18.0 2.0 %collective-permute-start.1 = (bf16[64,16,128]{2,1,0:T(8,128)(2,1)}, bf16[64,16,128]{2,1,0:T(8,128)(2,1)S(1)}, u32[]{:S(2)}, u32[]{:S(2)}) collective-permute-start(bf16[64,16,128]{2,1,0:T(8,128)(2,1)} %get-tuple-element.22), channel_id=1, source_target_pairs={{0,64},{64,128},{128,192},{192,0},{1,65},{65,129},{129,193},{193,1... | collective-permute-start | bytes 786440 | tf_op jit(solution)/shard_map/ppermute | solution.py:91
  20.0 1.4 %collective-permute-start.4 = (bf16[64,16,128]{2,1,0:T(8,128)(2,1)}, bf16[64,16,128]{2,1,0:T(8,128)(2,1)S(1)}, u32[]{:S(2)}, u32[]{:S(2)}) collective-permute-start(bf16[64,16,128]{2,1,0:T(8,128)(2,1)} %get-tuple-element.25), channel_id=1, source_target_pairs={{0,192},{64,0},{128,64},{192,128},{1,193},{65,1},{129,65},{193,129... | collective-permute-start | bytes 786440 | tf_op jit(solution)/shard_map/ppermute | solution.py:91
  21.4 1.4 %collective-permute-start = (bf16[64,16,128]{2,1,0:T(8,128)(2,1)}, bf16[64,16,128]{2,1,0:T(8,128)(2,1)S(1)}, u32[]{:S(2)}, u32[]{:S(2)}) collective-permute-start(bf16[64,16,128]{2,1,0:T(8,128)(2,1)} %get-tuple-element.20), channel_id=1, source_target_pairs={{0,192},{64,0},{128,64},{192,128},{1,193},{65,1},{129,65},{193,129... | collective-permute-start | bytes 786440 | tf_op jit(solution)/shard_map/ppermute | solution.py:92
  22.7 0.1 collective-permute-start.3
  22.8 16.8 %apply_class_1.1 = (f32[64,32,128]{2,1,0:T(8,128)}, bf16[64,16,128]{2,1,0:T(8,128)(2,1)}, bf16[64,16,128]{2,1,0:T(8,128)(2,1)}, bf16[64,16,128]{2,1,0:T(8,128)(2...) custom-call(s32[1]{0:T(128)} %bitcast.op_ref, ...), custom_call_target="tpu_custom_call" | custom-call | flops 2147483648 | bytes 8388608 | tf_op jit(solution)/shard_map/apply_class_1/pallas_call | solution.py:57
  39.6 2.7 %collective-permute-start.10 = (bf16[64,16,128]{2,1,0:T(8,128)(2,1)}, bf16[64,16,128]{2,1,0:T(8,128)(2,1)S(1)}, u32[]{:S(2)}, u32[]{:S(2)}) collective-permute-start(bf16[64,16,128]{2,1,0:T(8,128)(2,1)} %get-tuple-element.32), channel_id=1, source_target_pairs={{0,192},{64,0},{128,64},{192,128},{1,193},{65,1},{129,65},{193,129... | collective-permute-start | bytes 786440 | tf_op jit(solution)/shard_map/ppermute | solution.py:91
  42.4 0.1 collective-permute-start.2
  42.5 0.1 add_convert_fusion.5
  42.6 3.7 %collective-permute-done.10 = bf16[64,16,128]{2,1,0:T(8,128)(2,1)S(1)} collective-permute-done((bf16[64,16,128]{2,1,0:T(8,128)(2,1)}, bf16[64,16,128]{2,1,0:T(8,128)(2,1)S(1)}, u32[]{:S(2)}, u32[]{:S(2)}) %collective-permute-start.10) | collective-permute-done | bytes 262176 | tf_op jit(solution)/shard_map/ppermute | solution.py:91
  46.3 3.3 %collective-permute-start.5 = (bf16[64,16,128]{2,1,0:T(8,128)(2,1)S(1)}, bf16[64,16,128]{2,1,0:T(8,128)(2,1)S(1)}, u32[]{:S(2)}, u32[]{:S(2)}) collective-permute-start(bf16[64,16,128]{2,1,0:T(8,128)(2,1)S(1)} %add_convert_fusion.5), channel_id=1, source_target_pairs={{0,192},{64,0},{128,64},{192,128},{1,193},{65,1},{129,65},{193,129... | collective-permute-start | bytes 786440 | tf_op jit(solution)/shard_map/ppermute | solution.py:94
  49.6 1.1 add_convert_fusion.1
  50.7 0.1 collective-permute-start.6
  50.8 0.1 add_convert_fusion.3
  50.9 1.5 %collective-permute-start.9 = (bf16[64,16,128]{2,1,0:T(8,128)(2,1)S(1)}, bf16[64,16,128]{2,1,0:T(8,128)(2,1)S(1)}, u32[]{:S(2)}, u32[]{:S(2)}) collective-permute-start(bf16[64,16,128]{2,1,0:T(8,128)(2,1)S(1)} %copy-done.7), channel_id=1, source_target_pairs={{0,64},{64,128},{128,192},{192,0},{1,65},{65,129},{129,193},{193,1... | collective-permute-start | bytes 786440 | tf_op jit(solution)/shard_map/ppermute | solution.py:92
  52.4 1.2 %collective-permute-start.11 = (bf16[64,16,128]{2,1,0:T(8,128)(2,1)S(1)}, bf16[64,16,128]{2,1,0:T(8,128)(2,1)S(1)}, u32[]{:S(2)}, u32[]{:S(2)}) collective-permute-start(bf16[64,16,128]{2,1,0:T(8,128)(2,1)S(1)} %add_convert_fusion.1), channel_id=1, source_target_pairs={{0,192},{64,0},{128,64},{192,128},{1,193},{65,1},{129,65},{193,129... | collective-permute-start | bytes 786440 | tf_op jit(solution)/shard_map/ppermute | solution.py:94
  53.7 1.2 %collective-permute-done.2 = bf16[64,16,128]{2,1,0:T(8,128)(2,1)S(1)} collective-permute-done((bf16[64,16,128]{2,1,0:T(8,128)(2,1)S(1)}, bf16[64,16,128]{2,1,0:T(8,128)(2,1)S(1)}, u32[]{:S(2)}, u32[]{:S(2)}) %collective-permute-start.2) | collective-permute-done | bytes 262176 | tf_op jit(solution)/shard_map/ppermute | solution.py:93
  54.9 0.2 fusion
  55.1 3.8 %collective-permute-done.6 = bf16[64,16,128]{2,1,0:T(8,128)(2,1)S(1)} collective-permute-done((bf16[64,16,128]{2,1,0:T(8,128)(2,1)S(1)}, bf16[64,16,128]{2,1,0:T(8,128)(2,1)S(1)}, u32[]{:S(2)}, u32[]{:S(2)}) %collective-permute-start.6) | collective-permute-done | bytes 262176 | tf_op jit(solution)/shard_map/ppermute | solution.py:92
  59.0 1.6 %collective-permute-done.9 = bf16[64,16,128]{2,1,0:T(8,128)(2,1)S(1)} collective-permute-done((bf16[64,16,128]{2,1,0:T(8,128)(2,1)S(1)}, bf16[64,16,128]{2,1,0:T(8,128)(2,1)S(1)}, u32[]{:S(2)}, u32[]{:S(2)}) %collective-permute-start.9) | collective-permute-done | bytes 262176 | tf_op jit(solution)/shard_map/ppermute | solution.py:92
  60.6 4.0 %collective-permute-done.11 = bf16[64,16,128]{2,1,0:T(8,128)(2,1)S(1)} collective-permute-done((bf16[64,16,128]{2,1,0:T(8,128)(2,1)S(1)}, bf16[64,16,128]{2,1,0:T(8,128)(2,1)S(1)}, u32[]{:S(2)}, u32[]{:S(2)}) %collective-permute-start.11) | collective-permute-done | bytes 262176 | tf_op jit(solution)/shard_map/ppermute | solution.py:94
  64.6 1.6 %collective-permute-done.8 = bf16[64,16,128]{2,1,0:T(8,128)(2,1)S(1)} collective-permute-done((bf16[64,16,128]{2,1,0:T(8,128)(2,1)S(1)}, bf16[64,16,128]{2,1,0:T(8,128)(2,1)S(1)}, u32[]{:S(2)}, u32[]{:S(2)}) %collective-permute-start.8) | collective-permute-done | bytes 262176 | tf_op jit(solution)/shard_map/ppermute | solution.py:93
  66.2 0.2 fusion.2
  66.4 1.1 maximum_maximum_fusion
  67.4 14.8 %all-to-all-start = ((bf16[64,2,32,128]{3,2,1,0:T(8,128)(2,1)}), bf16[64,2,32,128]{3,2,1,0:T(8,128)(2,1)S(1)}, u32[]{:S(2)}, u32[]{:S(2)}) async-start(bf16[64,2,32,128]{3,2,1,0:T(8,128)(2,1)} %maximum_maximum_fusion), calls=%async_computation | async-start | bytes 2097152 | tf_op jit(solution)/shard_map/all_to_all | solution.py:116
  82.2 0.1 reshape.68
  82.3 0.7 fusion.6.slot_ref
  83.1 27.3 %all-to-all-done.arrived_ref = bf16[64,2,32,128]{3,2,1,0:T(8,128)(2,1)S(1)} async-done(((bf16[64,2,32,128]{3,2,1,0:T(8,128)(2,1)}), bf16[64,2,32,128]{3,2,1,0:T(8,128)(2,1)S(1)}, u32[]{:S(2)}, u32[]{:S(2)}) %all-to-all-start) | async-done | bytes 1048608 | tf_op jit(solution)/shard_map/all_to_all | solution.py:116
  110.4 1.0 copy-done
  111.4 3.4 %place_blocks.1 = f32[64,32,128]{2,1,0:T(8,128)} custom-call(s32[2,64]{1,0:T(2,128)} %fusion.6.slot_ref, bf16[64,2,32,128]{3,2,1,0:T(8,128)(2,1)} %copy-done), custom_call_target="tpu_custom_call" | custom-call | tf_op jit(solution)/shard_map/place_blocks/pallas_call | solution.py:118
  (26 shorter events, 0.1 us)
Async XLA Ops:
  18.0 24.3 %collective-permute-start.1 = (bf16[64,16,128]{2,1,0:T(8,128)(2,1)}, bf16[64,16,128]{2,1,0:T(8,128)(2,1)S(1)}, u32[]{:S(2)}, u32[]{:S(2)}) collective-permute-start(bf16[64,16,128]{2,1,0:T(8,128)(2,1)} %get-tuple-element.22), channel_id=1, source_target_pairs={{0,64},{64,128},{128,192},{192,0},{1,65},{65,129},{129,193},{193,1... | collective-permute-start | bytes 786440 | tf_op jit(solution)/shard_map/ppermute | solution.py:91
  20.0 22.4 %collective-permute-start.4 = (bf16[64,16,128]{2,1,0:T(8,128)(2,1)}, bf16[64,16,128]{2,1,0:T(8,128)(2,1)S(1)}, u32[]{:S(2)}, u32[]{:S(2)}) collective-permute-start(bf16[64,16,128]{2,1,0:T(8,128)(2,1)} %get-tuple-element.25), channel_id=1, source_target_pairs={{0,192},{64,0},{128,64},{192,128},{1,193},{65,1},{129,65},{193,129... | collective-permute-start | bytes 786440 | tf_op jit(solution)/shard_map/ppermute | solution.py:91
  21.4 29.5 %collective-permute-start = (bf16[64,16,128]{2,1,0:T(8,128)(2,1)}, bf16[64,16,128]{2,1,0:T(8,128)(2,1)S(1)}, u32[]{:S(2)}, u32[]{:S(2)}) collective-permute-start(bf16[64,16,128]{2,1,0:T(8,128)(2,1)} %get-tuple-element.20), channel_id=1, source_target_pairs={{0,192},{64,0},{128,64},{192,128},{1,193},{65,1},{129,65},{193,129... | collective-permute-start | bytes 786440 | tf_op jit(solution)/shard_map/ppermute | solution.py:92
  22.7 29.7 %collective-permute-start.3 = (bf16[64,16,128]{2,1,0:T(8,128)(2,1)}, bf16[64,16,128]{2,1,0:T(8,128)(2,1)S(1)}, u32[]{:S(2)}, u32[]{:S(2)}) collective-permute-start(bf16[64,16,128]{2,1,0:T(8,128)(2,1)} %get-tuple-element.23), channel_id=1, source_target_pairs={{0,64},{64,128},{128,192},{192,0},{1,65},{65,129},{129,193},{193,1... | collective-permute-start | bytes 786440 | tf_op jit(solution)/shard_map/ppermute | solution.py:92
  22.8 19.5 %copy-start.5 = (bf16[64,16,128]{2,1,0:T(8,128)(2,1)S(1)}, bf16[64,16,128]{2,1,0:T(8,128)(2,1)}, u32[]{:S(2)}) copy-start(bf16[64,16,128]{2,1,0:T(8,128)(2,1)} %get-tuple-element.21) | copy-start | bytes 786436
  22.8 19.7 %copy-start.3 = (bf16[64,16,128]{2,1,0:T(8,128)(2,1)S(1)}, bf16[64,16,128]{2,1,0:T(8,128)(2,1)}, u32[]{:S(2)}) copy-start(bf16[64,16,128]{2,1,0:T(8,128)(2,1)} %get-tuple-element.24) | copy-start | bytes 786436
  39.6 11.1 %copy-start.8 = (bf16[64,16,128]{2,1,0:T(8,128)(2,1)S(1)}, bf16[64,16,128]{2,1,0:T(8,128)(2,1)}, u32[]{:S(2)}) copy-start(bf16[64,16,128]{2,1,0:T(8,128)(2,1)} %get-tuple-element.27) | copy-start | bytes 786436
  39.6 11.2 %copy-start.4 = (bf16[64,16,128]{2,1,0:T(8,128)(2,1)S(1)}, bf16[64,16,128]{2,1,0:T(8,128)(2,1)}, u32[]{:S(2)}) copy-start(bf16[64,16,128]{2,1,0:T(8,128)(2,1)} %get-tuple-element.28) | copy-start | bytes 786436
  39.6 11.3 %copy-start.7 = (bf16[64,16,128]{2,1,0:T(8,128)(2,1)S(1)}, bf16[64,16,128]{2,1,0:T(8,128)(2,1)}, u32[]{:S(2)}) copy-start(bf16[64,16,128]{2,1,0:T(8,128)(2,1)} %get-tuple-element.30) | copy-start | bytes 786436
  39.6 15.3 %copy-start.1 = (f32[64,32,128]{2,1,0:T(8,128)S(1)}, f32[64,32,128]{2,1,0:T(8,128)}, u32[]{:S(2)}) copy-start(f32[64,32,128]{2,1,0:T(8,128)} %get-tuple-element.19) | copy-start | bytes 3145732
  39.6 6.6 %collective-permute-start.10 = (bf16[64,16,128]{2,1,0:T(8,128)(2,1)}, bf16[64,16,128]{2,1,0:T(8,128)(2,1)S(1)}, u32[]{:S(2)}, u32[]{:S(2)}) collective-permute-start(bf16[64,16,128]{2,1,0:T(8,128)(2,1)} %get-tuple-element.32), channel_id=1, source_target_pairs={{0,192},{64,0},{128,64},{192,128},{1,193},{65,1},{129,65},{193,129... | collective-permute-start | bytes 786440 | tf_op jit(solution)/shard_map/ppermute | solution.py:91
  42.3 8.4 %collective-permute-start.7 = (bf16[64,16,128]{2,1,0:T(8,128)(2,1)}, bf16[64,16,128]{2,1,0:T(8,128)(2,1)S(1)}, u32[]{:S(2)}, u32[]{:S(2)}) collective-permute-start(bf16[64,16,128]{2,1,0:T(8,128)(2,1)} %get-tuple-element.29), channel_id=1, source_target_pairs={{0,64},{64,128},{128,192},{192,0},{1,65},{65,129},{129,193},{193,1... | collective-permute-start | bytes 786440 | tf_op jit(solution)/shard_map/ppermute | solution.py:91
  42.4 12.5 %collective-permute-start.2 = (bf16[64,16,128]{2,1,0:T(8,128)(2,1)S(1)}, bf16[64,16,128]{2,1,0:T(8,128)(2,1)S(1)}, u32[]{:S(2)}, u32[]{:S(2)}) collective-permute-start(bf16[64,16,128]{2,1,0:T(8,128)(2,1)S(1)} %add_convert_fusion.7), channel_id=1, source_target_pairs={{0,64},{64,128},{128,192},{192,0},{1,65},{65,129},{129,193},{193,1... | collective-permute-start | bytes 786440 | tf_op jit(solution)/shard_map/ppermute | solution.py:93
  46.3 8.7 %collective-permute-start.5 = (bf16[64,16,128]{2,1,0:T(8,128)(2,1)S(1)}, bf16[64,16,128]{2,1,0:T(8,128)(2,1)S(1)}, u32[]{:S(2)}, u32[]{:S(2)}) collective-permute-start(bf16[64,16,128]{2,1,0:T(8,128)(2,1)S(1)} %add_convert_fusion.5), channel_id=1, source_target_pairs={{0,192},{64,0},{128,64},{192,128},{1,193},{65,1},{129,65},{193,129... | collective-permute-start | bytes 786440 | tf_op jit(solution)/shard_map/ppermute | solution.py:94
  49.6 16.6 %copy-start.2 = (f32[64,32,128]{2,1,0:T(8,128)S(1)}, f32[64,32,128]{2,1,0:T(8,128)}, u32[]{:S(2)}) copy-start(f32[64,32,128]{2,1,0:T(8,128)} %get-tuple-element.26) | copy-start | bytes 3145732
  50.7 8.2 %collective-permute-start.6 = (bf16[64,16,128]{2,1,0:T(8,128)(2,1)S(1)}, bf16[64,16,128]{2,1,0:T(8,128)(2,1)S(1)}, u32[]{:S(2)}, u32[]{:S(2)}) collective-permute-start(bf16[64,16,128]{2,1,0:T(8,128)(2,1)S(1)} %copy-done.8), channel_id=1, source_target_pairs={{0,192},{64,0},{128,64},{192,128},{1,193},{65,1},{129,65},{193,129... | collective-permute-start | bytes 786440 | tf_op jit(solution)/shard_map/ppermute | solution.py:92
  50.9 9.6 %collective-permute-start.9 = (bf16[64,16,128]{2,1,0:T(8,128)(2,1)S(1)}, bf16[64,16,128]{2,1,0:T(8,128)(2,1)S(1)}, u32[]{:S(2)}, u32[]{:S(2)}) collective-permute-start(bf16[64,16,128]{2,1,0:T(8,128)(2,1)S(1)} %copy-done.7), channel_id=1, source_target_pairs={{0,64},{64,128},{128,192},{192,0},{1,65},{65,129},{129,193},{193,1... | collective-permute-start | bytes 786440 | tf_op jit(solution)/shard_map/ppermute | solution.py:92
  52.4 12.1 %collective-permute-start.11 = (bf16[64,16,128]{2,1,0:T(8,128)(2,1)S(1)}, bf16[64,16,128]{2,1,0:T(8,128)(2,1)S(1)}, u32[]{:S(2)}, u32[]{:S(2)}) collective-permute-start(bf16[64,16,128]{2,1,0:T(8,128)(2,1)S(1)} %add_convert_fusion.1), channel_id=1, source_target_pairs={{0,192},{64,0},{128,64},{192,128},{1,193},{65,1},{129,65},{193,129... | collective-permute-start | bytes 786440 | tf_op jit(solution)/shard_map/ppermute | solution.py:94
  54.9 11.2 %collective-permute-start.8 = (bf16[64,16,128]{2,1,0:T(8,128)(2,1)S(1)}, bf16[64,16,128]{2,1,0:T(8,128)(2,1)S(1)}, u32[]{:S(2)}, u32[]{:S(2)}) collective-permute-start(bf16[64,16,128]{2,1,0:T(8,128)(2,1)S(1)} %add_convert_fusion.3), channel_id=1, source_target_pairs={{0,64},{64,128},{128,192},{192,0},{1,65},{65,129},{129,193},{193,1... | collective-permute-start | bytes 786440 | tf_op jit(solution)/shard_map/ppermute | solution.py:93
  66.3 15.9 %copy-start.6 = (s32[2,4096]{1,0:T(2,128)S(1)}, s32[2,4096]{1,0:T(2,128)}, u32[]{:S(2)}) copy-start(s32[2,4096]{1,0:T(2,128)} %param.11) | copy-start | bytes 98308
  67.4 43.0 %all-to-all-start = ((bf16[64,2,32,128]{3,2,1,0:T(8,128)(2,1)}), bf16[64,2,32,128]{3,2,1,0:T(8,128)(2,1)S(1)}, u32[]{:S(2)}, u32[]{:S(2)}) async-start(bf16[64,2,32,128]{3,2,1,0:T(8,128)(2,1)} %maximum_maximum_fusion), calls=%async_computation | async-start | bytes 2097152 | tf_op jit(solution)/shard_map/all_to_all | solution.py:116
  110.4 1.0 copy-start

commit v2 on v0

v2 whole, which is shorter than its diff:
```python
import functools

import jax
import jax.numpy as jnp
from jax import lax
from jax.experimental import pallas as pl
from jax.experimental.pallas import tpu as pltpu
from jax.sharding import PartitionSpec as P


F32, BF16 = jnp.float32, jnp.bfloat16
GROUP = 32
PARTS = (((0, 16), (16, 16)), ((0, 32),))
JOINED = (((0, 0),), ((0, 1),), ((1, 0),))
BATCHES = (((0, 0), (0, 1)), ((1, 0),))
MIB = 1 << 20


def apply_kernel(target_hbm, lsec_hbm, rsec_hbm, wave_hbm, left_hbm, right_hbm, *refs, q, per):
    outs, (wave, left, right, mixed_ref, target, lsec, rsec, small_sem, left_sem, right_sem, wave_sem) = refs[:-11], refs[-11:]
    blocks, rows, cols = wave.shape
    terms = left.shape[0]
    op_size = rows // per
    own_op, own_sec = lax.axis_index("op"), lax.axis_index("sec")
    width = target.shape[1]
    window = pl.multiple_of(own_sec * blocks // width * width, width)
    first = lax.rem(own_sec * blocks, width)
    small = [
        pltpu.make_async_copy(target_hbm.at[:, pl.ds(window, width)], target, small_sem.at[0]),
        pltpu.make_async_copy(lsec_hbm, lsec, small_sem.at[1]),
        pltpu.make_async_copy(rsec_hbm, rsec, small_sem.at[2]),
    ]
    lefts = [pltpu.make_async_copy(left_hbm.at[q, t], left.at[t], left_sem.at[t]) for t in range(terms)]
    rights = [pltpu.make_async_copy(right_hbm.at[q, t], right.at[t], right_sem.at[t]) for t in range(terms)]

    def wave_copy(g):
        part = pl.ds(g * GROUP, GROUP)
        return pltpu.make_async_copy(wave_hbm.at[part], wave.at[part], wave_sem.at[g])

    for copy in small + lefts:
        copy.start()
    wave_copy(0).start()
    for copy in rights:
        copy.start()
    for g in range(1, blocks // GROUP):
        wave_copy(g).start()
    offsets = [pl.multiple_of(lax.rem(own_op + r, op_size) * per, per) for r in range(op_size)]
    for copy in small + lefts:
        copy.wait()

    def step(g, carry):
        wave_copy(g).wait()
        for i in range(GROUP):
            b = g * GROUP + i
            ls = lsec[b]
            stacked = jnp.concatenate([left[t, ls, pl.ds(off, per), :] for t in range(terms) for off in offsets], axis=0)
            mixed = jnp.dot(stacked, wave[b], preferred_element_type=F32).astype(BF16)
            for t in range(terms):
                mixed_ref[i, :, t * cols : (t + 1) * cols] = mixed[t * rows : (t + 1) * rows]

        @pl.when(g == 0)
        def _():
            for copy in rights:
                copy.wait()

        for i in range(GROUP):
            b = g * GROUP + i
            rs = rsec[b]
            place = target[q, first + b] // blocks
            rhs = jnp.concatenate([right[t, rs] for t in range(terms)], axis=1)
            acc = lax.dot_general(mixed_ref[i], rhs, (((1,), (1,)), ((), ())), preferred_element_type=F32)
            low = place < blocks // 2
            for k, (start, count) in enumerate(PARTS[q]):
                own, first_up, first_down, second = outs[4 * k : 4 * k + 4]
                zero, one, two, three = (acc[r * per + start : r * per + start + count] for r in range(op_size))
                one, two, three = (v.astype(BF16) for v in (one, two, three))
                own[place] = zero
                first_up[place] = jnp.where(low, two, one)
                first_down[place] = jnp.where(low, three, two)
                second[place] = jnp.where(low, one, three)
        return carry

    lax.fori_loop(0, blocks // GROUP, step, 0)


def apply_class(q, target, left_sector, right_sector, wavefunction, left_ops, right_ops):
    blocks, rows, cols = wavefunction.shape
    _, terms, sectors, _, _ = left_ops.shape
    per = rows // lax.axis_size("op")
    width = max(blocks, 128)
    outs = [
        pltpu.VMEM((blocks, count, cols), t) for _, count in PARTS[q] for t in (F32, BF16, BF16, BF16)
    ]
    flops = 2 * blocks * terms * (rows * rows * cols + rows * cols * cols)
    return pl.pallas_call(
        functools.partial(apply_kernel, q=q, per=per),
        out_shape=outs,
        in_specs=[pl.BlockSpec(memory_space=pltpu.HBM)] * 6,
        out_specs=[pl.BlockSpec(memory_space=pltpu.VMEM) for _ in outs],
        scratch_shapes=[
            pltpu.VMEM(wavefunction.shape, BF16),
            pltpu.VMEM((terms, sectors, rows, rows), BF16),
            pltpu.VMEM((terms, right_ops.shape[2], cols, cols), BF16),
            pltpu.VMEM((GROUP, rows, terms * cols), BF16),
            pltpu.SMEM((target.shape[0], width), jnp.int32),
            pltpu.SMEM(left_sector.shape, jnp.int32),
            pltpu.SMEM(right_sector.shape, jnp.int32),
            pltpu.SemaphoreType.DMA((3,)),
            pltpu.SemaphoreType.DMA((terms,)),
            pltpu.SemaphoreType.DMA((terms,)),
            pltpu.SemaphoreType.DMA((blocks // GROUP,)),
        ],
        compiler_params=pltpu.CompilerParams(vmem_limit_bytes=24 * MIB),
        cost_estimate=pl.CostEstimate(flops=flops, bytes_accessed=8 * MIB, transcendentals=0),
    )(*(pltpu.with_memory_space_constraint(a, pltpu.HBM) for a in (target, left_sector, right_sector, wavefunction, left_ops, right_ops)))


def shift(value, step, op_size):
    ring = [(i, (i + step) % op_size) for i in range(op_size)]
    return lax.ppermute(value, "op", ring)


def add(a, b):
    return (a.astype(F32) + b.astype(F32)).astype(BF16)


def place_kernel(source, *refs, layout, classes):
    arrived, out_hbm, out, out_sem = refs[:-3], *refs[-3:]
    blocks = out.shape[0]
    steps = out_sem.shape[0]
    chunk = blocks // steps

    def out_copy(c):
        part = pl.ds(c * chunk, chunk)
        return pltpu.make_async_copy(out.at[part], out_hbm.at[part], out_sem.at[c])

    def step(c, carry):
        for i in range(chunk):
            slot = c * chunk + i
            sources = [source[q, slot] for q in range(classes)]
            rows = {}
            for batch, row, (q, start, rows_here) in layout:
                for k in range(0, rows_here, 16):
                    term = arrived[batch][sources[q], row + k : row + k + 16].astype(F32)
                    rows.setdefault(start + k, []).append(term)
            for start, terms in rows.items():
                out[slot, start : start + 16] = functools.reduce(lambda a, b: a + b, terms)
        out_copy(c).start()
        return carry

    lax.fori_loop(0, steps, step, 0)
    for c in range(steps):
        out_copy(c).wait()


def per_device(wavefunction, left_ops, right_ops, left_sector, right_sector, target):
    shards = lax.axis_size("sec")
    op_size = lax.axis_size("op")
    own_sec = lax.axis_index("sec")
    blocks, rows, cols = wavefunction.shape
    classes = target.shape[0]
    per = rows // op_size
    operands = (target, left_sector, right_sector, wavefunction, left_ops, right_ops)
    parts = {}
    for q in range(classes):
        outs = apply_class(q, *operands)
        for k in range(len(PARTS[q])):
            parts[q, k] = outs[4 * k : 4 * k + 4]
    half = blocks // 2
    first = {key: (shift(up, 1, op_size), shift(down, -1, op_size)) for key, (_, up, down, _) in parts.items()}
    join = lambda values: values[0] if len(values) == 1 else jnp.concatenate(values, axis=1)
    summed = {}
    for group in JOINED:
        low = shift(join([add(parts[k][3][:half], first[k][0][:half]) for k in group]), 1, op_size)
        high = shift(join([add(parts[k][3][half:], first[k][1][half:]) for k in group]), -1, op_size)
        row = 0
        for key in group:
            rows_here = slice(row, row + PARTS[key[0]][key[1]][1])
            own, below, above = parts[key][0], *first[key]
            summed[key] = jnp.concatenate(
                [
                    own[:half] + above[:half].astype(F32) + low[:, rows_here].astype(F32),
                    own[half:] + below[half:].astype(F32) + high[:, rows_here].astype(F32),
                ],
                axis=0,
            ).astype(BF16)
            row = rows_here.stop
    arrived, layout = [], []
    for n, batch in enumerate(BATCHES):
        row = 0
        for q, k in batch:
            layout.append((n, row, (q, *PARTS[q][k])))
            row += PARTS[q][k][1]
        arrived.append(
            lax.all_to_all(join([summed[key] for key in batch]), "sec", split_axis=0, concat_axis=0, tiled=True)
        )
    by_source = target.reshape(classes, shards, blocks)
    slots = jnp.sum(jnp.where(by_source // blocks == own_sec, by_source % blocks, 0), axis=2)
    sources = jnp.sum(
        jnp.where(slots[:, None, :] == jnp.arange(blocks)[None, :, None], jnp.arange(shards, dtype=jnp.int32), 0), axis=2
    )
    sources = jnp.minimum(sources, shards - 1)
    steps = 4
    return pl.pallas_call(
        functools.partial(place_kernel, layout=layout, classes=classes),
        out_shape=jax.ShapeDtypeStruct((blocks, per, cols), F32),
        in_specs=[pl.BlockSpec(memory_space=pltpu.SMEM)] + [pl.BlockSpec(memory_space=pltpu.VMEM)] * len(arrived),
        out_specs=pl.BlockSpec(memory_space=pltpu.HBM),
        scratch_shapes=[pltpu.VMEM((blocks, per, cols), F32), pltpu.SemaphoreType.DMA((steps,))],
        compiler_params=pltpu.CompilerParams(vmem_limit_bytes=16 * MIB),
        name="place_blocks",
    )(sources, *arrived)


def solution(mesh):
    in_specs = (
        P("sec", None, None),
        P(None, "op", None, None, None),
        P(None, "op", None, None, None),
        P("sec"),
        P("sec"),
        P(),
    )

    return jax.shard_map(per_device, mesh=mesh, in_specs=in_specs, out_specs=P("sec", "op", None), check_vma=False)
```

time: 347 us -> 103 us (0.30)
  waiting for transfers between devices: 171 us -> 45.4 us
  matrix products: 58.7 us -> 0 us
  local copies, waits for them, and re-layouts: 58.7 us -> 0.11 us
  other arithmetic: 23.9 us -> 4.7 us
  starting transfers between devices: 20.5 us -> 36.9 us
  Pallas kernels: 0 us -> 15.3 us
  between operations: 13.6 us -> 0.3 us
    all_to_all x2, waiting for transfers between devices: 124 us -> 23 us  [per_device(): lax.all_to_all(join([summed[key] for key in batch]), 'sec', split_axis=0,...]
    dot_general x8 -> x0, matrix products: 58.7 us -> none  [add_term(): jnp.einsum('bik,blk->bil', left_mixed, right_blocks, preferred_element_ty...]
    reduce_scatter x1 -> x0, waiting for transfers between devices: 46.8 us -> none  [per_device(): return lax.psum_scatter(partial_sum, 'op', scatter_dimension=1, tiled=True)]
    gather x20 -> x0, local copies, waits for them, and re-layouts: 44.7 us -> none  [the longest x8 17.3 us: add_term(): left_blocks = jnp.take(left_term, left_sector, axis=0)]
    ppermute x0 -> x12, waiting for transfers between devices: none -> 22.4 us  [shift(): return lax.ppermute(value, 'op', ring)]
    pallas_call x0 -> x3, Pallas kernels: none -> 15.3 us  [the longest x2 13.7 us: apply_class(): pl.pallas_call(functools.partial(apply_kernel, q=q, per=per), out_shape=o...]
    ppermute x0 -> x12, starting transfers between devices: none -> 14.5 us  [shift(): return lax.ppermute(value, 'op', ring)]
    squeeze x11 -> x0, local copies, waits for them, and re-layouts: 13 us -> none  [the longest x8 8.52 us: class_terms(): running, _ = lax.scan(add_term, initial, (left_ops, right_ops))]
  transfers between devices with their start and end apart: 3 -> 14, of which waited for: 3 -> 6; matrix products, arithmetic and copies ran while one was open for 19% -> 5% of each run, Pallas kernels for 0% -> 7%
where the time goes in v2:
time: 103 us
  waiting for transfers between devices  45.4 us (44%)
  starting transfers between devices  36.9 us (36%)
  Pallas kernels  15.3 us (15%)
  other arithmetic  4.7 us (5%)
    all_to_all x2, waiting for transfers between devices, per_device(): lax.all_to_all(join([summed[key] for key in batch]), 'sec', split_axis=0,...  23 us
    all_to_all x2, starting transfers between devices, per_device(): lax.all_to_all(join([summed[key] for key in batch]), 'sec', split_axis=0,...  22.4 us
    ppermute x12, waiting for transfers between devices, shift(): return lax.ppermute(value, 'op', ring)  22.4 us
    ppermute x12, starting transfers between devices, shift(): return lax.ppermute(value, 'op', ring)  14.5 us
    pallas_call x2, Pallas kernels, apply_class(): pl.pallas_call(functools.partial(apply_kernel, q=q, per=per), out_shape=o...  13.7 us
  transfers between devices with their start and end apart: 14, of which 6 were waited for; matrix products, arithmetic and copies ran while one was open for 5% of the time, Pallas kernels for 7%

profile of v2, /device:TPU:1, one launch (start us, length us, event | category | flops | bytes accessed | tf_op | source)
XLA Modules:
  0.0 102.7 jit_solution(6640347404987053319)
XLA Ops:
  0.0 6.9 %shard_map.64 = (f32[64,16,128]{2,1,0:T(8,128)S(1)}, bf16[64,16,128]{2,1,0:T(8,128)(2,1)S(1)}, bf16[64,16,128]{2,1,0:T(8,128)(2,1)S(1)}, bf16[64,16,128]{2,1,0:T...) custom-call(s32[2,4096]{1,0:T(2,128)} %target_hbm.3, ...), custom_call_target="tpu_custom_call" | custom-call | flops 2147483648 | bytes 8388608 | tf_op jit(solution)/shard_map/pallas_call | solution.py:95
  6.9 3.4 %collective-permute-start = (bf16[64,16,128]{2,1,0:T(8,128)(2,1)S(1)}, bf16[64,16,128]{2,1,0:T(8,128)(2,1)S(1)}, u32[]{:S(2)}, u32[]{:S(2)}) collective-permute-start(bf16[64,16,128]{2,1,0:T(8,128)(2,1)S(1)} %get-tuple-element.18), channel_id=1, source_target_pairs={{0,192},{64,0},{128,64},{192,128},{1,193},{65,1},{129,65},{193,129... | collective-permute-start | bytes 786440 | tf_op jit(solution)/shard_map/ppermute | solution.py:120
  10.3 2.7 %collective-permute-start.4 = (bf16[64,16,128]{2,1,0:T(8,128)(2,1)S(1)}, bf16[64,16,128]{2,1,0:T(8,128)(2,1)S(1)}, u32[]{:S(2)}, u32[]{:S(2)}) collective-permute-start(bf16[64,16,128]{2,1,0:T(8,128)(2,1)S(1)} %get-tuple-element.22), channel_id=1, source_target_pairs={{0,192},{64,0},{128,64},{192,128},{1,193},{65,1},{129,65},{193,129... | collective-permute-start | bytes 786440 | tf_op jit(solution)/shard_map/ppermute | solution.py:120
  12.9 0.0 collective-permute-start.5
  12.9 6.9 %shard_map.65 = (f32[64,32,128]{2,1,0:T(8,128)S(1)}, bf16[64,32,128]{2,1,0:T(8,128)(2,1)S(1)}, bf16[64,32,128]{2,1,0:T(8,128)(2,1)S(1)}, bf16[64,32,128]{2,1,0:T(8,128)(2,1)S(1)}) custom-call(s32[2,4096]{1,0:T(2,128)} %target_hbm.3, s32[64]{0:T(128)} %lsec_hbm.3, s32[64]{0:T(128)} %rsec_hbm.3, bf16[64,128,128]{2,1,0:T(8,128)(2,1)} %wave_hbm.3, ...), custom_call_target="tpu_custom_call" | custom-call | flops 2147483648 | bytes 8388608 | tf_op jit(solution)/shard_map/pallas_call | solution.py:95
  19.8 2.8 %collective-permute-start.8 = (bf16[64,32,128]{2,1,0:T(8,128)(2,1)S(1)}, bf16[64,32,128]{2,1,0:T(8,128)(2,1)}, u32[]{:S(2)}, u32[]{:S(2)}) collective-permute-start(bf16[64,32,128]{2,1,0:T(8,128)(2,1)S(1)} %get-tuple-element.26), channel_id=1, source_target_pairs={{0,192},{64,0},{128,64},{192,128},{1,193},{65,1},{129,65},{193,129... | collective-permute-start | bytes 1572872 | tf_op jit(solution)/shard_map/ppermute | solution.py:120
  22.6 0.1 add_convert_fusion.11
  22.7 0.1 collective-permute-start.2
  22.8 2.7 %collective-permute-start.3 = (bf16[32,16,128]{2,1,0:T(8,128)(2,1)S(1)}, bf16[32,16,128]{2,1,0:T(8,128)(2,1)S(1)}, u32[]{:S(2)}, u32[]{:S(2)}) collective-permute-start(bf16[32,16,128]{2,1,0:T(8,128)(2,1)S(1)} %get-tuple-element.38), channel_id=1, source_target_pairs={{0,192},{64,0},{128,64},{192,128},{1,193},{65,1},{129,65},{193,129... | collective-permute-start | bytes 393224 | tf_op jit(solution)/shard_map/ppermute | solution.py:120
  25.5 0.1 add_convert_fusion.7
  25.6 0.1 collective-permute-start.6
  25.7 12.4 %collective-permute-done.2 = bf16[32,16,128]{2,1,0:T(8,128)(2,1)S(1)} collective-permute-done((bf16[32,16,128]{2,1,0:T(8,128)(2,1)S(1)}, bf16[32,16,128]{2,1,0:T(8,128)(2,1)S(1)}, u32[]{:S(2)}, u32[]{:S(2)}) %collective-permute-start.2) | collective-permute-done | bytes 131104 | tf_op jit(solution)/shard_map/ppermute | solution.py:120
  38.1 0.0 collective-permute-start.7
  38.1 0.1 add_convert_fusion.10
  38.2 2.6 %collective-permute-done.6 = bf16[32,16,128]{2,1,0:T(8,128)(2,1)S(1)} collective-permute-done((bf16[32,16,128]{2,1,0:T(8,128)(2,1)S(1)}, bf16[32,16,128]{2,1,0:T(8,128)(2,1)S(1)}, u32[]{:S(2)}, u32[]{:S(2)}) %collective-permute-start.6) | collective-permute-done | bytes 131104 | tf_op jit(solution)/shard_map/ppermute | solution.py:120
  40.8 1.4 %collective-permute-done.7 = bf16[32,16,128]{2,1,0:T(8,128)(2,1)S(1)} collective-permute-done((bf16[32,16,128]{2,1,0:T(8,128)(2,1)S(1)}, bf16[32,16,128]{2,1,0:T(8,128)(2,1)S(1)}, u32[]{:S(2)}, u32[]{:S(2)}) %collective-permute-start.7) | collective-permute-done | bytes 131104 | tf_op jit(solution)/shard_map/ppermute | solution.py:120
  42.2 0.1 add_convert_fusion.6
  42.3 0.8 maximum_maximum_fusion
  43.2 16.7 %all-to-all-start = ((bf16[64,32,128]{2,1,0:T(8,128)(2,1)}), bf16[64,32,128]{2,1,0:T(8,128)(2,1)S(1)}, u32[]{:S(2)}, u32[]{:S(2)}) async-start(bf16[64,32,128]{2,1,0:T(8,128)(2,1)} %maximum_maximum_fusion), calls=%async_computation | async-start | bytes 1048576 | tf_op jit(solution)/shard_map/all_to_all | solution.py:195
  59.9 1.2 %add_convert_fusion.3 = (bf16[32,32,128]{2,1,0:T(8,128)(2,1)S(1)}, bf16[32,32,128]{2,1,0:T(8,128)(2,1)S(1)}) fusion(bf16[64,32,128]{2,1,0:T(8,128)(2,1)} %collective-permute-done.9, bf16[64,32,128]{2,1,0:T(8,128)(2,1)S(1)} %get-tuple-element.27, bf16[64,32,128]{2,1,0:T(8,128)(2,1)} %collective-permute-done.8), kind=kLoop, calls=%fused_computation.5 | loop fusion | flops 1048576 | bytes 1572864 | tf_op jit(solution)/shard_map/convert_element_type | solution.py:124
  61.1 0.1 collective-permute-start.10
  61.2 2.7 %collective-permute-start.11 = (bf16[32,32,128]{2,1,0:T(8,128)(2,1)S(1)}, bf16[32,32,128]{2,1,0:T(8,128)(2,1)S(1)}, u32[]{:S(2)}, u32[]{:S(2)}) collective-permute-start(bf16[32,32,128]{2,1,0:T(8,128)(2,1)S(1)} %get-tuple-element.32), channel_id=1, source_target_pairs={{0,192},{64,0},{128,64},{192,128},{1,193},{65,1},{129,65},{193,129... | collective-permute-start | bytes 786440 | tf_op jit(solution)/shard_map/ppermute | solution.py:120
  63.8 5.9 %collective-permute-done.10 = bf16[32,32,128]{2,1,0:T(8,128)(2,1)S(1)} collective-permute-done((bf16[32,32,128]{2,1,0:T(8,128)(2,1)S(1)}, bf16[32,32,128]{2,1,0:T(8,128)(2,1)S(1)}, u32[]{:S(2)}, u32[]{:S(2)}) %collective-permute-start.10) | collective-permute-done | bytes 262176 | tf_op jit(solution)/shard_map/ppermute | solution.py:120
  69.8 1.3 %add_convert_fusion.2 = (bf16[32,32,128]{2,1,0:T(8,128)(2,1)S(1)}, bf16[32,32,128]{2,1,0:T(8,128)(2,1)S(1)}) fusion(bf16[32,32,128]{2,1,0:T(8,128)(2,1)S(1)} %collective-permute-done.10, f32[64,32,128]{2,1,0:T(8,128)S(1)} %get-tuple-element.25, bf16[64,32,128]{2,1,0:T(8,128)(2,1)} %collective-permute-done.8, ...), kind=kLoop, calls=%fused_computation.4 | loop fusion | flops 1310720 | bytes 2621440 | tf_op jit(solution)/shard_map/convert
  71.1 0.8 pad_maximum_fusion
  71.9 5.7 %all-to-all-done.refs_0_ = bf16[64,32,128]{2,1,0:T(8,128)(2,1)S(1)} async-done(((bf16[64,32,128]{2,1,0:T(8,128)(2,1)}), bf16[64,32,128]{2,1,0:T(8,128)(2,1)S(1)}, u32[]{:S(2)}, u32[]{:S(2)}) %all-to-all-start) | async-done | bytes 524320 | tf_op jit(solution)/shard_map/all_to_all | solution.py:195
  77.6 5.7 %all-to-all-start.1 = ((bf16[64,32,128]{2,1,0:T(8,128)(2,1)}), bf16[64,32,128]{2,1,0:T(8,128)(2,1)S(1)}, u32[]{:S(2)}, u32[]{:S(2)}) async-start(bf16[64,32,128]{2,1,0:T(8,128)(2,1)} %pad_maximum_fusion), calls=%async_computation.1 | async-start | bytes 1048576 | tf_op jit(solution)/shard_map/all_to_all | solution.py:195
  83.3 0.1 reshape.4
  83.4 0.2 fusion.2
  83.6 0.1 select_reduce_fusion
  83.7 17.3 %all-to-all-done.1.refs_1_ = bf16[64,32,128]{2,1,0:T(8,128)(2,1)S(1)} async-done(((bf16[64,32,128]{2,1,0:T(8,128)(2,1)}), bf16[64,32,128]{2,1,0:T(8,128)(2,1)S(1)}, u32[]{:S(2)}, u32[]{:S(2)}) %all-to-all-start.1) | async-done | bytes 524320 | tf_op jit(solution)/shard_map/all_to_all | solution.py:195
  101.0 1.6 %place_blocks.1 = f32[64,32,128]{2,1,0:T(8,128)} custom-call(s32[2,64]{1,0:T(2,128)S(1)} %broadcast_minimum_fusion.source, bf16[64,32,128]{2,1,0:T(8,128)(2,1)S(1)} %all-to-all-done.refs_0_, bf16[64,32,128]{2,1,0:T(8,128)(2,1)S(1)} %all-to-all-done.1.refs_1_), custom_call_target="tpu_custom_call" | custom-call | tf_op jit(solution)/shard_map/place_blocks/pallas_call | solution.py:204
  (13 shorter events, 0.0 us)
Async XLA Ops:
  6.9 15.7 %collective-permute-start = (bf16[64,16,128]{2,1,0:T(8,128)(2,1)S(1)}, bf16[64,16,128]{2,1,0:T(8,128)(2,1)S(1)}, u32[]{:S(2)}, u32[]{:S(2)}) collective-permute-start(bf16[64,16,128]{2,1,0:T(8,128)(2,1)S(1)} %get-tuple-element.18), channel_id=1, source_target_pairs={{0,192},{64,0},{128,64},{192,128},{1,193},{65,1},{129,65},{193,129... | collective-permute-start | bytes 786440 | tf_op jit(solution)/shard_map/ppermute | solution.py:120
  10.3 12.3 %collective-permute-start.1 = (bf16[64,16,128]{2,1,0:T(8,128)(2,1)S(1)}, bf16[64,16,128]{2,1,0:T(8,128)(2,1)S(1)}, u32[]{:S(2)}, u32[]{:S(2)}) collective-permute-start(bf16[64,16,128]{2,1,0:T(8,128)(2,1)S(1)} %get-tuple-element.20), channel_id=1, source_target_pairs={{0,64},{64,128},{128,192},{192,0},{1,65},{65,129},{129,193},{193,1... | collective-permute-start | bytes 786440 | tf_op jit(solution)/shard_map/ppermute | solution.py:120
  10.3 12.5 %collective-permute-start.4 = (bf16[64,16,128]{2,1,0:T(8,128)(2,1)S(1)}, bf16[64,16,128]{2,1,0:T(8,128)(2,1)S(1)}, u32[]{:S(2)}, u32[]{:S(2)}) collective-permute-start(bf16[64,16,128]{2,1,0:T(8,128)(2,1)S(1)} %get-tuple-element.22), channel_id=1, source_target_pairs={{0,192},{64,0},{128,64},{192,128},{1,193},{65,1},{129,65},{193,129... | collective-permute-start | bytes 786440 | tf_op jit(solution)/shard_map/ppermute | solution.py:120
  12.9 12.6 %collective-permute-start.5 = (bf16[64,16,128]{2,1,0:T(8,128)(2,1)S(1)}, bf16[64,16,128]{2,1,0:T(8,128)(2,1)S(1)}, u32[]{:S(2)}, u32[]{:S(2)}) collective-permute-start(bf16[64,16,128]{2,1,0:T(8,128)(2,1)S(1)} %get-tuple-element.24), channel_id=1, source_target_pairs={{0,64},{64,128},{128,192},{192,0},{1,65},{65,129},{129,193},{193,1... | collective-permute-start | bytes 786440 | tf_op jit(solution)/shard_map/ppermute | solution.py:120
  19.8 40.1 %collective-permute-start.8 = (bf16[64,32,128]{2,1,0:T(8,128)(2,1)S(1)}, bf16[64,32,128]{2,1,0:T(8,128)(2,1)}, u32[]{:S(2)}, u32[]{:S(2)}) collective-permute-start(bf16[64,32,128]{2,1,0:T(8,128)(2,1)S(1)} %get-tuple-element.26), channel_id=1, source_target_pairs={{0,192},{64,0},{128,64},{192,128},{1,193},{65,1},{129,65},{193,129... | collective-permute-start | bytes 1572872 | tf_op jit(solution)/shard_map/ppermute | solution.py:120
  22.6 37.3 %collective-permute-start.9 = (bf16[64,32,128]{2,1,0:T(8,128)(2,1)S(1)}, bf16[64,32,128]{2,1,0:T(8,128)(2,1)}, u32[]{:S(2)}, u32[]{:S(2)}) collective-permute-start(bf16[64,32,128]{2,1,0:T(8,128)(2,1)S(1)} %get-tuple-element.28), channel_id=1, source_target_pairs={{0,64},{64,128},{128,192},{192,0},{1,65},{65,129},{129,193},{193,1... | collective-permute-start | bytes 1572872 | tf_op jit(solution)/shard_map/ppermute | solution.py:120
  22.7 15.4 %collective-permute-start.2 = (bf16[32,16,128]{2,1,0:T(8,128)(2,1)S(1)}, bf16[32,16,128]{2,1,0:T(8,128)(2,1)S(1)}, u32[]{:S(2)}, u32[]{:S(2)}) collective-permute-start(bf16[32,16,128]{2,1,0:T(8,128)(2,1)S(1)} %get-tuple-element.37), channel_id=1, source_target_pairs={{0,64},{64,128},{128,192},{192,0},{1,65},{65,129},{129,193},{193,1... | collective-permute-start | bytes 393224 | tf_op jit(solution)/shard_map/ppermute | solution.py:120
  22.8 15.4 %collective-permute-start.3 = (bf16[32,16,128]{2,1,0:T(8,128)(2,1)S(1)}, bf16[32,16,128]{2,1,0:T(8,128)(2,1)S(1)}, u32[]{:S(2)}, u32[]{:S(2)}) collective-permute-start(bf16[32,16,128]{2,1,0:T(8,128)(2,1)S(1)} %get-tuple-element.38), channel_id=1, source_target_pairs={{0,192},{64,0},{128,64},{192,128},{1,193},{65,1},{129,65},{193,129... | collective-permute-start | bytes 393224 | tf_op jit(solution)/shard_map/ppermute | solution.py:120
  25.6 15.2 %collective-permute-start.6 = (bf16[32,16,128]{2,1,0:T(8,128)(2,1)S(1)}, bf16[32,16,128]{2,1,0:T(8,128)(2,1)S(1)}, u32[]{:S(2)}, u32[]{:S(2)}) collective-permute-start(bf16[32,16,128]{2,1,0:T(8,128)(2,1)S(1)} %get-tuple-element.39), channel_id=1, source_target_pairs={{0,64},{64,128},{128,192},{192,0},{1,65},{65,129},{129,193},{193,1... | collective-permute-start | bytes 393224 | tf_op jit(solution)/shard_map/ppermute | solution.py:120
  38.1 4.1 %collective-permute-start.7 = (bf16[32,16,128]{2,1,0:T(8,128)(2,1)S(1)}, bf16[32,16,128]{2,1,0:T(8,128)(2,1)S(1)}, u32[]{:S(2)}, u32[]{:S(2)}) collective-permute-start(bf16[32,16,128]{2,1,0:T(8,128)(2,1)S(1)} %get-tuple-element.40), channel_id=1, source_target_pairs={{0,192},{64,0},{128,64},{192,128},{1,193},{65,1},{129,65},{193,129... | collective-permute-start | bytes 393224 | tf_op jit(solution)/shard_map/ppermute | solution.py:120
  43.2 34.4 %all-to-all-start = ((bf16[64,32,128]{2,1,0:T(8,128)(2,1)}), bf16[64,32,128]{2,1,0:T(8,128)(2,1)S(1)}, u32[]{:S(2)}, u32[]{:S(2)}) async-start(bf16[64,32,128]{2,1,0:T(8,128)(2,1)} %maximum_maximum_fusion), calls=%async_computation | async-start | bytes 1048576 | tf_op jit(solution)/shard_map/all_to_all | solution.py:195
  61.1 8.7 %collective-permute-start.10 = (bf16[32,32,128]{2,1,0:T(8,128)(2,1)S(1)}, bf16[32,32,128]{2,1,0:T(8,128)(2,1)S(1)}, u32[]{:S(2)}, u32[]{:S(2)}) collective-permute-start(bf16[32,32,128]{2,1,0:T(8,128)(2,1)S(1)} %get-tuple-element.31), channel_id=1, source_target_pairs={{0,64},{64,128},{128,192},{192,0},{1,65},{65,129},{129,193},{193,1... | collective-permute-start | bytes 786440 | tf_op jit(solution)/shard_map/ppermute | solution.py:120
  61.2 8.6 %collective-permute-start.11 = (bf16[32,32,128]{2,1,0:T(8,128)(2,1)S(1)}, bf16[32,32,128]{2,1,0:T(8,128)(2,1)S(1)}, u32[]{:S(2)}, u32[]{:S(2)}) collective-permute-start(bf16[32,32,128]{2,1,0:T(8,128)(2,1)S(1)} %get-tuple-element.32), channel_id=1, source_target_pairs={{0,192},{64,0},{128,64},{192,128},{1,193},{65,1},{129,65},{193,129... | collective-permute-start | bytes 786440 | tf_op jit(solution)/shard_map/ppermute | solution.py:120
  69.8 13.5 %copy-start = (s32[2,4096]{1,0:T(2,128)S(1)}, s32[2,4096]{1,0:T(2,128)}, u32[]{:S(2)}) copy-start(s32[2,4096]{1,0:T(2,128)} %target_hbm.3) | copy-start | bytes 98308
  77.6 23.4 %all-to-all-start.1 = ((bf16[64,32,128]{2,1,0:T(8,128)(2,1)}), bf16[64,32,128]{2,1,0:T(8,128)(2,1)S(1)}, u32[]{:S(2)}, u32[]{:S(2)}) async-start(bf16[64,32,128]{2,1,0:T(8,128)(2,1)} %pad_maximum_fusion), calls=%async_computation.1 | async-start | bytes 1048576 | tf_op jit(solution)/shard_map/all_to_all | solution.py:195
